TPU v7x, 32 devices: a whole 2x2x4 slice. The times are simulated.
32 devices in a mesh: dp: 8 (over y, x, core), tensor: 4 (over z).
Axes of the slice: x: 2, y: 2, z: 4, core: 2. Of those that a mesh axis runs over, the one named last changes fastest.
Arguments:
- tokens: bfloat16 [8192, 768], P(('dp', 'tensor')), may hold values from -6 to 6
- segments: int32 [8192], P('dp'), may hold values from 0 to 3, as said below
- buckets: int32 [1024], replicated, may hold values from 0 to 31, as said below
- routes: int32 [8192, 2], P(('dp', 'tensor')), may hold values from 0 to 7, all different within a row; in each aligned block of 256 rows (0 to 255, 256 to 511, ...) at most 128 rows name the same one
- norm_one: float32 [768], replicated, may hold values from 0.5 to 1.5
- w_qkv: bfloat16 [768, 3, 768], P(None, None, 'tensor'), may hold values from -0.21875 to 0.21875
- w_out: bfloat16 [768, 768], P('tensor'), may hold values from -0.625 to 0.625
- rel_bias: float32 [32, 12], P(None, 'tensor'), may hold values from -4 to 4
- norm_two: float32 [768], replicated, may hold values from 0.5 to 1.5
- w_router: bfloat16 [768, 8], replicated, may hold values from -0.21875 to 0.21875
- w_gate: bfloat16 [8, 768, 3072], P('dp', None, 'tensor'), may hold values from -0.21875 to 0.21875
- w_up: bfloat16 [8, 768, 3072], P('dp', None, 'tensor'), may hold values from -0.21875 to 0.21875
- w_down: bfloat16 [8, 3072, 768], P('dp', 'tensor'), may hold values from -0.875 to 0.875
- cotangent: bfloat16 [8192, 768], P(('dp', 'tensor')), may hold values from -6 to 6
Outputs:
- mixed_out: bfloat16 [8192, 768], P(('dp', 'tensor'))
- grad_tokens: bfloat16 [8192, 768], P(('dp', 'tensor'))
- grad_norm_one: float32 [768], replicated
- grad_qkv: float32 [768, 3, 768], P(None, None, 'tensor')
- grad_out: float32 [768, 768], P('tensor')
- grad_bias: float32 [32, 12], P(None, 'tensor')
- grad_norm_two: float32 [768], replicated
- grad_router: float32 [768, 8], replicated
- grad_gate: float32 [8, 768, 3072], P('dp', None, 'tensor')
- grad_up: float32 [8, 768, 3072], P('dp', None, 'tensor')
- grad_down: float32 [8, 3072, 768], P('dp', 'tensor')
Inputs may be any that keep to these rules, and one draw needn't show every extreme that they name: `segments`: within each block of 1024 slots of one index of dp the ids start at 0, never fall and rise by one from a sequence to the next; a sequence is a run of equal ids; in every draw some block holds a single sequence of 1024 tokens and some block four sequences. `buckets`: starts at 0, never falls, rises by at most one from a distance to the next, and ends at 31. `routes`: each row names 2 different experts; in each aligned block of 256 rows (the rows of one device) no expert is named by more than 128 rows, a bound that some block reaches.
All inputs are finite; a program needn't handle non-finite values.
Results may differ from a plain program's by a relative error of at most 0.025.
Values may be sent and summed in bfloat16 or wider, within the bound.
A program may use at most 192 MiB of HBM per device.

v0:
```python
import jax
import jax.numpy as jnp
from jax import lax
from jax.sharding import PartitionSpec as P

HD = 64
EPSILON = 1e-06
HIGHEST = lax.Precision.HIGHEST


def contract(left, right, left_dim, right_dim):
    return lax.dot_general(
        left, right, (((left_dim,), (right_dim,)), ((), ())), preferred_element_type=jnp.float32
    )


def gated(pre_gate, pre_up):
    return jax.nn.gelu(pre_gate, approximate=True) * pre_up


def carry_out(buffer):
    grouped = lax.all_gather(buffer, "tensor", axis=1, tiled=True)
    return lax.all_to_all(grouped, "dp", split_axis=0, concat_axis=0, tiled=True)


def carry_back(partial_rows):
    returned = lax.all_to_all(partial_rows, "dp", split_axis=0, concat_axis=0, tiled=True)
    return lax.psum_scatter(
        returned.astype(jnp.float32).astype(jnp.bfloat16), "tensor", scatter_dimension=1, tiled=True
    ).astype(jnp.float32)


def bucket_edges(buckets, bucket_count):
    bucket_ids = jnp.arange(bucket_count, dtype=jnp.int32)
    lower = jnp.sum((buckets[None, :] < bucket_ids[:, None]).astype(jnp.int32), axis=1)
    upper = jnp.concatenate([lower[1:], jnp.full((1,), buckets.shape[0], jnp.int32)])
    return (lower, upper)


def block_scores(query_block, key, first, segments, lower, upper, rel_bias, scale):
    count = query_block.shape[0]
    length = key.shape[0]
    distance = (first + jnp.arange(count, dtype=jnp.int32))[:, None] - jnp.arange(
        length, dtype=jnp.int32
    )[None, :]
    allowed = (distance >= 0) & (segments[first : first + count][:, None] == segments[None, :])
    reach = jnp.maximum(distance, 0)[:, :, None]
    onehot = ((reach >= lower[None, None, :]) & (reach < upper[None, None, :])).astype(jnp.float32)
    bias = jnp.einsum("ijb,bh->hij", onehot, rel_bias, precision=HIGHEST)
    scores = (
        jnp.einsum("ihd,jhd->hij", query_block, key, preferred_element_type=jnp.float32) * scale
        + bias
    )
    masked = jnp.where(allowed[None], scores, -1e30)
    return (masked, allowed, onehot)


def local(
    tokens,
    segments,
    buckets,
    routes,
    norm_one,
    w_qkv,
    w_out,
    rel_bias,
    norm_two,
    w_router,
    w_gate,
    w_up,
    w_down,
    cotangent,
):
    rows_dev = tokens.shape[0]
    width = tokens.shape[1]
    tok_dev = segments.shape[0]
    bucket_count = rel_bias.shape[0]
    heads_local = rel_bias.shape[1]
    inner = heads_local * HD
    experts = w_router.shape[1]
    groups = lax.axis_size("tensor")
    dp_count = lax.axis_size("dp")
    capacity = 4 * tok_dev // (groups * experts)
    top = routes.shape[1]
    pair_count = rows_dev * top
    block = min(512, tok_dev)
    scale = HD ** (-0.5)
    values = tokens.astype(jnp.float32)
    inverse_one = lax.rsqrt(jnp.mean(values * values, axis=1, keepdims=True) + EPSILON)
    scaled_one = values * inverse_one
    normed_one = (scaled_one * norm_one).astype(jnp.bfloat16)
    normed_all = lax.all_gather(normed_one, "tensor", axis=0, tiled=True)
    proj_weight = w_qkv.reshape(width, 3 * inner)
    projected = jnp.dot(normed_all, proj_weight, preferred_element_type=jnp.float32).astype(
        jnp.bfloat16
    )
    query = projected[:, :inner].reshape(tok_dev, heads_local, HD)
    key = projected[:, inner : 2 * inner].reshape(tok_dev, heads_local, HD)
    value = projected[:, 2 * inner :].reshape(tok_dev, heads_local, HD)
    lower, upper = bucket_edges(buckets, bucket_count)
    contexts = []
    logsums = []
    for first in range(0, tok_dev, block):
        masked, allowed, onehot = block_scores(
            query[first : first + block], key, first, segments, lower, upper, rel_bias, scale
        )
        peak = jnp.max(masked, axis=2, keepdims=True)
        logsum = peak + jnp.log(jnp.sum(jnp.exp(masked - peak), axis=2, keepdims=True))
        probs = jnp.where(allowed[None], jnp.exp(masked - logsum), 0.0)
        probs_low = probs.astype(jnp.bfloat16)
        context_block = jnp.einsum(
            "hij,jhd->ihd", probs_low, value, preferred_element_type=jnp.float32
        )
        contexts.append(context_block.astype(jnp.bfloat16).reshape(block, inner))
        logsums.append(logsum)
    context = jnp.concatenate(contexts, axis=0)
    rows = context
    attended = lax.psum_scatter(
        jnp.dot(rows, w_out, preferred_element_type=jnp.float32).astype(jnp.bfloat16),
        "tensor",
        scatter_dimension=0,
        tiled=True,
    ).astype(jnp.float32)
    hidden = values + attended
    inverse_two = lax.rsqrt(jnp.mean(hidden * hidden, axis=1, keepdims=True) + EPSILON)
    scaled_two = hidden * inverse_two
    normed_two = (scaled_two * norm_two).astype(jnp.bfloat16)
    logits = jnp.dot(normed_two, w_router, preferred_element_type=jnp.float32)
    router = jax.nn.softmax(logits, axis=1)
    choose = (routes[:, :, None] == jnp.arange(experts, dtype=jnp.int32)[None, None, :]).astype(
        jnp.float32
    )
    gate_vals = jnp.sum(choose * router[:, None, :], axis=2)
    expert_ids = routes.reshape(-1)
    member = (expert_ids[:, None] == jnp.arange(experts, dtype=jnp.int32)[None, :]).astype(
        jnp.int32
    )
    earlier = jnp.cumsum(member, axis=0) - member
    place = jnp.sum(earlier * member, axis=1)
    slot = expert_ids * capacity + place
    owner = (
        jnp.full((experts * capacity,), -1, dtype=jnp.int32)
        .at[slot]
        .set(jnp.arange(pair_count, dtype=jnp.int32))
    )
    filled = (owner >= 0)[:, None]
    owner_pair = jnp.maximum(owner, 0)
    send_rows = jnp.where(filled, normed_two[owner_pair // top], 0).reshape(
        experts, capacity, width
    )
    rows_in = carry_out(send_rows).reshape(-1, width)
    gate_weight = w_gate[0]
    up_weight = w_up[0]
    down_weight = w_down[0]
    pre_gate = jnp.dot(rows_in, gate_weight, preferred_element_type=jnp.float32)
    pre_up = jnp.dot(rows_in, up_weight, preferred_element_type=jnp.float32)
    active = gated(pre_gate, pre_up).astype(jnp.bfloat16)
    partial_rows = jnp.dot(active, down_weight, preferred_element_type=jnp.float32).astype(
        jnp.bfloat16
    )
    back_slots = carry_back(partial_rows.reshape(dp_count, groups * capacity, width)).reshape(
        experts * capacity, width
    )
    pair_out = back_slots[slot].reshape(rows_dev, top, width)
    mixed = hidden + jnp.sum(gate_vals[:, :, None] * pair_out, axis=1)
    upstream = cotangent.astype(jnp.float32)
    grad_gates = jnp.sum(upstream[:, None, :] * pair_out, axis=2)
    grad_pairs = (
        (gate_vals[:, :, None] * upstream[:, None, :])
        .astype(jnp.bfloat16)
        .reshape(pair_count, width)
    )
    send_grads = jnp.where(filled, grad_pairs[owner_pair], 0).reshape(experts, capacity, width)
    grad_in = carry_out(send_grads).reshape(-1, width)
    grad_active = contract(grad_in, down_weight, 1, 1)
    grad_down = contract(active, grad_in, 0, 0)
    unused, pull = jax.vjp(gated, pre_gate, pre_up)
    grad_pre_gate, grad_pre_up = pull(grad_active)
    grad_pre_gate = grad_pre_gate.astype(jnp.bfloat16)
    grad_pre_up = grad_pre_up.astype(jnp.bfloat16)
    grad_gate = contract(rows_in, grad_pre_gate, 0, 0)
    grad_up = contract(rows_in, grad_pre_up, 0, 0)
    grad_rows_x = (
        contract(grad_pre_gate, gate_weight, 1, 1) + contract(grad_pre_up, up_weight, 1, 1)
    ).astype(jnp.bfloat16)
    grad_slots = carry_back(grad_rows_x.reshape(dp_count, groups * capacity, width)).reshape(
        experts * capacity, width
    )
    grad_pair_rows = grad_slots[slot].reshape(rows_dev, top, width)
    grad_router_probs = jnp.sum(choose * grad_gates[:, :, None], axis=1)
    grad_logits = (
        router * (grad_router_probs - jnp.sum(router * grad_router_probs, axis=1, keepdims=True))
    ).astype(jnp.bfloat16)
    grad_router = contract(normed_two, grad_logits, 0, 0)
    grad_normed_two = jnp.sum(grad_pair_rows, axis=1) + contract(grad_logits, w_router, 1, 1)
    grad_norm_two = jnp.sum(grad_normed_two * scaled_two, axis=0)
    spread_two = grad_normed_two * norm_two
    grad_hidden = upstream + inverse_two * (
        spread_two - scaled_two * jnp.mean(spread_two * scaled_two, axis=1, keepdims=True)
    )
    grad_attended = grad_hidden.astype(jnp.bfloat16)
    piece = lax.all_gather(grad_attended, "tensor", axis=0, tiled=True)
    rows = context
    grad_out_sum = contract(rows, piece, 0, 0)
    grad_piece = contract(piece, w_out, 1, 1)
    grad_context_all = grad_piece
    grad_out_local, grad_context_all = (grad_out_sum, grad_context_all)
    grad_context = grad_context_all.astype(jnp.bfloat16).reshape(tok_dev, heads_local, HD)
    query_grads = []
    grad_key = jnp.zeros((tok_dev, heads_local, HD), jnp.float32)
    grad_value = jnp.zeros((tok_dev, heads_local, HD), jnp.float32)
    grad_bias_local = jnp.zeros((bucket_count, heads_local), jnp.float32)
    for index, first in enumerate(range(0, tok_dev, block)):
        masked, allowed, onehot = block_scores(
            query[first : first + block], key, first, segments, lower, upper, rel_bias, scale
        )
        probs = jnp.where(allowed[None], jnp.exp(masked - logsums[index]), 0.0)
        probs_low = probs.astype(jnp.bfloat16)
        grad_block = grad_context[first : first + block]
        grad_probs = jnp.einsum(
            "ihd,jhd->hij", grad_block, value, preferred_element_type=jnp.float32
        )
        row_delta = jnp.sum(probs * grad_probs, axis=2, keepdims=True)
        grad_scores = (probs * (grad_probs - row_delta)).astype(jnp.bfloat16)
        query_grads.append(
            jnp.einsum("hij,jhd->ihd", grad_scores, key, preferred_element_type=jnp.float32) * scale
        )
        grad_key = (
            grad_key
            + jnp.einsum(
                "hij,ihd->jhd",
                grad_scores,
                query[first : first + block],
                preferred_element_type=jnp.float32,
            )
            * scale
        )
        grad_value = grad_value + jnp.einsum(
            "hij,ihd->jhd", probs_low, grad_block, preferred_element_type=jnp.float32
        )
        grad_bias_local = grad_bias_local + jnp.einsum(
            "hij,ijb->bh", grad_scores.astype(jnp.float32), onehot, precision=HIGHEST
        )
    grad_query = jnp.concatenate(query_grads, axis=0)
    grad_proj_rows = jnp.concatenate(
        [
            grad_query.reshape(tok_dev, inner),
            grad_key.reshape(tok_dev, inner),
            grad_value.reshape(tok_dev, inner),
        ],
        axis=1,
    ).astype(jnp.bfloat16)
    grad_qkv_local = contract(normed_all, grad_proj_rows, 0, 0).reshape(width, 3, inner)
    rows = grad_proj_rows
    grad_normed_one = lax.psum_scatter(
        contract(rows, proj_weight, 1, 1).astype(jnp.bfloat16),
        "tensor",
        scatter_dimension=0,
        tiled=True,
    ).astype(jnp.float32)
    grad_norm_one = jnp.sum(grad_normed_one * scaled_one, axis=0)
    spread_one = grad_normed_one * norm_one
    grad_tokens = grad_hidden + inverse_one * (
        spread_one - scaled_one * jnp.mean(spread_one * scaled_one, axis=1, keepdims=True)
    )
    grad_qkv_sum, grad_out_sum, grad_bias_sum = lax.psum(
        (grad_qkv_local, grad_out_local, grad_bias_local), "dp"
    )
    grad_router_sum, grad_two_sum, grad_one_sum = lax.psum(
        (grad_router, grad_norm_two, grad_norm_one), ("dp", "tensor")
    )
    return (
        mixed.astype(jnp.bfloat16),
        grad_tokens.astype(jnp.bfloat16),
        grad_one_sum,
        grad_qkv_sum,
        grad_out_sum,
        grad_bias_sum,
        grad_two_sum,
        grad_router_sum,
        grad_gate[None],
        grad_up[None],
        grad_down[None],
    )


def solution(mesh):
    return jax.shard_map(
        local,
        mesh=mesh,
        in_specs=(
            P(("dp", "tensor"), None),
            P("dp"),
            P(),
            P(("dp", "tensor"), None),
            P(),
            P(None, None, "tensor"),
            P("tensor", None),
            P(None, "tensor"),
            P(),
            P(),
            P("dp", None, "tensor"),
            P("dp", None, "tensor"),
            P("dp", "tensor", None),
            P(("dp", "tensor"), None),
        ),
        out_specs=(
            P(("dp", "tensor"), None),
            P(("dp", "tensor"), None),
            P(),
            P(None, None, "tensor"),
            P("tensor", None),
            P(None, "tensor"),
            P(),
            P(),
            P("dp", None, "tensor"),
            P("dp", None, "tensor"),
            P("dp", "tensor", None),
        ),
        check_vma=False,
    )
```

profile of v0, /device:TPU:0, one launch (start us, length us, event | category | flops | bytes accessed | tf_op | source)
XLA Modules:
  0.0 987.0 jit_solution(7135961302743151335)
XLA Ops:
  9.1 1.9 fusion.69
  12.3 25.9 %fusion.3 = f32[512,1024,3]{1,2,0:T(4,128)} fusion(s32[512,1024]{1,0:T(8,128)S(1)} %fusion.29, s32[32]{0:T(128)S(1)} %pad_add_fusion, s32[32]{0:T(128)S(1)} %convert_reduce_fusion, f32[32,3]{0,1:T(4,128)} %param.21), kind=kOutput, calls=%fused_computation.10 | convolution fusion | flops 654311424 | bytes 8389248 | tf_op jit(solution)/shard_map/ijb,bh->hij/dot_general | solution.py:49
  40.0 25.4 %fusion.1 = f32[512,1024,3]{1,2,0:T(4,128)} fusion(s32[512,1024]{1,0:T(8,128)S(1)} %fusion.31, s32[32]{0:T(128)S(1)} %pad_add_fusion, s32[32]{0:T(128)S(1)} %convert_reduce_fusion, f32[32,3]{0,1:T(4,128)S(1)} %copy-done.60), kind=kOutput, calls=%fused_computation.8 | convolution fusion | flops 654311424 | bytes 8389248 | tf_op jit(solution)/shard_map/ijb,bh->hij/dot_general | solution.py:49
  65.4 2.5 convolution_convert_fusion.3
  68.1 8.4 fusion.105
  76.5 1.5 exponential_reduce_fusion
  78.1 5.0 fusion.106
  83.1 1.9 exponential_reduce_fusion.1
  85.1 1.5 convolution_convert_fusion.5
  86.7 1.5 convolution_convert_fusion.6
  88.9 1.8 convolution_convert_fusion.2
  91.2 1.5 mul.287
  92.7 3.1 mul.288
  97.7 2.4 scatter_custom_fusion
  100.2 28.7 %reduce-scatter.5.cloned.1.call-done = bf16[256,768]{1,0:T(8,128)(2,1)} async-done(((bf16[1024,768]{1,0:T(8,128)(2,1)}), bf16[256,768]{1,0:T(8,128)(2,1)}) %reduce-scatter.5.cloned.1.call-update) | async-done | bytes 393232 | tf_op jit(solution)/shard_map/reduce_scatter | solution.py:118
  131.9 5.2 gather_fusion
  137.2 1.6 multiply_convert_fusion.4
  138.7 5.2 gather_fusion.2
  143.9 3.8 broadcast_select_fusion
  148.4 113.8 %all-gather.7.cloned.1.call-done = bf16[8,512,768]{2,1,0:T(8,128)(2,1)} async-done(((bf16[8,128,768]{2,1,0:T(8,128)(2,1)}), bf16[8,512,768]{2,1,0:T(8,128)(2,1)}) %all-gather.7.cloned.1.call-update) | async-done | bytes 6291472 | tf_op jit(solution)/shard_map/all_gather | solution.py:22
  262.2 4.8 all-to-all-start
  267.1 110.7 %all-gather.9.cloned.1.call-done = bf16[8,512,768]{2,1,0:T(8,128)(2,1)} async-done(((bf16[8,128,768]{2,1,0:T(8,128)(2,1)}), bf16[8,512,768]{2,1,0:T(8,128)(2,1)}) %all-gather.9.cloned.1.call-update) | async-done | bytes 6291472 | tf_op jit(solution)/shard_map/all_gather | solution.py:22
  377.8 4.8 all-to-all-start.2
  382.6 10.4 %fusion.46 = f32[4096,768]{1,0:T(8,128)} fusion(bf16[4096,768]{1,0:T(8,128)(2,1)} %bitcast.18, bf16[1,768,768]{2,1,0:T(8,128)(2,1)} %param.25), kind=kOutput, calls=%fused_computation.95 | convolution fusion | flops 4831838208 | bytes 20054016 | tf_op jit(solution)/shard_map/dot_general | solution.py:156
  393.0 10.5 %fusion.50 = f32[4096,768]{1,0:T(8,128)} fusion(bf16[4096,768]{1,0:T(8,128)(2,1)} %bitcast.18, bf16[1,768,768]{2,1,0:T(8,128)(2,1)S(1)} %copy-done.56), kind=kOutput, calls=%fused_computation.99 | convolution fusion | flops 4831838208 | bytes 20054016 | tf_op jit(solution)/shard_map/dot_general | solution.py:155
  403.5 50.6 %all-to-all-done.2 = bf16[8,512,768]{2,1,0:T(8,128)(2,1)} async-done(((bf16[8,512,768]{2,1,0:T(8,128)(2,1)}), bf16[8,512,768]{2,1,0:T(8,128)(2,1)}, u32[]{:S(2)}, u32[]{:S(2)}) %all-to-all-start.2) | async-done | bytes 6291488 | tf_op jit(solution)/shard_map/all_to_all | solution.py:23
  454.2 21.3 %multiply_convert_fusion = (bf16[4096,768]{1,0:T(8,128)(2,1)}, bf16[4096,768]{1,0:T(8,128)(2,1)}, bf16[4096,768]{1,0:T(8,128)(2,1)S(1)}) fusion(f32[4096,768]{1,0:T(8,128)} %fusion.50, f32[4096,768]{1,0:T(8,128)} %fusion.46, bf16[4096,768]{1,0:T(8,128)(2,1)} %bitcast.25, bf16[1,768,768]{2,1,0:T(8,128)(2,1)S(1)} %copy-done), kind=kOutput, calls=%fused_computation.33 | convolution fusion | flops 4913627136 | bytes 51511296 | tf_op jit(solution)/shard_map/dot_general | solution.py:12
  475.5 5.3 convolution_convert_fusion
  480.7 74.9 %all_to_all.20 = bf16[8,512,768]{2,1,0:T(8,128)(2,1)} all-to-all(bf16[8,512,768]{2,1,0:T(8,128)(2,1)S(1)} %bitcast.146), channel_id=1, replica_groups=mesh['dp'=8,'tensor'=4] {'dp'}, dimensions={0} | all-to-all | bytes 12582912 | tf_op jit(solution)/shard_map/all_to_all | solution.py:27
  555.7 11.8 %fusion.48 = f32[4096,768]{1,0:T(8,128)} fusion(bf16[4096,768]{1,0:T(8,128)(2,1)} %get-tuple-element.23, bf16[1,768,768]{2,1,0:T(8,128)(2,1)S(1)} %copy-done.56), kind=kOutput, calls=%fused_computation.97 | convolution fusion | flops 4831838208 | bytes 20054016 | tf_op jit(solution)/shard_map/dot_general | solution.py:12
  567.5 10.1 %add_convert_fusion = bf16[4096,768]{1,0:T(8,128)(2,1)S(1)} fusion(f32[4096,768]{1,0:T(8,128)} %fusion.48, bf16[4096,768]{1,0:T(8,128)(2,1)} %get-tuple-element.22, bf16[1,768,768]{2,1,0:T(8,128)(2,1)S(1)} %copy-done.57), kind=kOutput, calls=%fused_computation.32 | convolution fusion | flops 4838129664 | bytes 26345472 | tf_op jit(solution)/shard_map/dot_general | solution.py:12
  577.6 74.9 %all_to_all.21 = bf16[8,512,768]{2,1,0:T(8,128)(2,1)} all-to-all(bf16[8,512,768]{2,1,0:T(8,128)(2,1)S(1)} %bitcast.145), channel_id=1, replica_groups=mesh['dp'=8,'tensor'=4] {'dp'}, dimensions={0} | all-to-all | bytes 12582912 | tf_op jit(solution)/shard_map/all_to_all | solution.py:27
  652.7 10.3 %reduce-scatter.7.cloned.1.call-done = bf16[8,128,768]{2,1,0:T(8,128)(2,1)} async-done(((bf16[8,512,768]{2,1,0:T(8,128)(2,1)}), bf16[8,128,768]{2,1,0:T(8,128)(2,1)}) %reduce-scatter.7.cloned.1.call-update) | async-done | bytes 1572880 | tf_op jit(solution)/shard_map/reduce_scatter | solution.py:28
  663.0 3.3 bitcast_convert_fusion.1
  666.3 5.1 gather_fusion.1
  671.3 3.3 reshape.354
  674.7 5.0 multiply_reduce_fusion.2
  679.8 96.7 %reduce-scatter.9.cloned.1.call-done = bf16[8,128,768]{2,1,0:T(8,128)(2,1)} async-done(((bf16[8,512,768]{2,1,0:T(8,128)(2,1)}), bf16[8,128,768]{2,1,0:T(8,128)(2,1)}) %reduce-scatter.9.cloned.1.call-update) | async-done | bytes 1572880 | tf_op jit(solution)/shard_map/reduce_scatter | solution.py:28
  776.5 3.3 bitcast_convert_fusion
  779.8 5.1 gather_fusion.3
  784.9 3.1 reshape.359
  788.0 3.3 reduce_sum.183
  793.0 10.2 %convolution_bitcast_fusion = f32[1,768,768]{2,1,0:T(8,128)} fusion(bf16[4096,768]{1,0:T(8,128)(2,1)} %copy-done.63, bf16[4096,768]{1,0:T(8,128)(2,1)} %bitcast.25), kind=kOutput, calls=%fused_computation.62 | convolution fusion | flops 4831838208 | bytes 14942208 | tf_op jit(solution)/shard_map/dot_general | solution.py:12
  803.2 10.1 %convolution_bitcast_fusion.1 = f32[1,768,768]{2,1,0:T(8,128)} fusion(bf16[4096,768]{1,0:T(8,128)(2,1)} %bitcast.18, bf16[4096,768]{1,0:T(8,128)(2,1)} %get-tuple-element.22), kind=kOutput, calls=%fused_computation.63 | convolution fusion | flops 4831838208 | bytes 14942208 | tf_op jit(solution)/shard_map/dot_general | solution.py:12
  813.3 17.3 %all-gather.11.cloned.1.call-done = bf16[1024,768]{1,0:T(8,128)(2,1)} async-done(((bf16[256,768]{1,0:T(8,128)(2,1)}), bf16[1024,768]{1,0:T(8,128)(2,1)}) %all-gather.11.cloned.1.call-update) | async-done | bytes 1572880 | tf_op jit(solution)/shard_map/all_gather | solution.py:202
  830.7 2.1 convolution_convert_fusion.4
  832.9 6.4 multiply_reduce_fusion.1
  839.3 6.4 multiply_reduce_fusion
  845.7 7.5 multiply_convert_fusion.2
  853.2 4.2 fusion.55
  857.4 2.7 fusion.108
  860.2 1.4 fusion.78
  863.4 1.5 fusion.37
  865.0 2.6 convolution_convert_fusion.1
  867.7 10.5 %convolution_bitcast_fusion.2 = f32[1,768,768]{2,1,0:T(8,128)} fusion(bf16[4096,768]{1,0:T(8,128)(2,1)} %bitcast.18, bf16[4096,768]{1,0:T(8,128)(2,1)} %get-tuple-element.23), kind=kOutput, calls=%fused_computation.64 | convolution fusion | flops 4831838208 | bytes 14942208 | tf_op jit(solution)/shard_map/dot_general | solution.py:12
  879.7 2.3 fusion.74
  882.9 17.2 %fusion.56 = f32[32,3]{0,1:T(4,128)S(1)} fusion(bf16[3,512,1024]{2,1,0:T(8,128)(2,1)S(1)} %copy-done.7, s32[512,1024]{1,0:T(8,128)S(1)} %copy-done.26, s32[32]{0:T(128)S(1)} %copy-done.62, s32[32]{0:T(128)S(1)} %copy-done.54), kind=kOutput, calls=%fused_computation.107 | convolution fusion | flops 150994944 | bytes 5243520 | tf_op jit(solution)/shard_map/hij,ijb->bh/dot_general | solution.py:241
  900.2 17.7 %fusion.62 = f32[32,3]{0,1:T(4,128)S(1)} fusion(f32[32,3]{0,1:T(4,128)S(1)} %fusion.56, bf16[3,512,1024]{2,1,0:T(8,128)(2,1)} %get-tuple-element.53, s32[512,1024]{1,0:T(8,128)} %copy-done.27, s32[32]{0:T(128)S(1)} %copy-done.62, s32[32]{0:T(128)S(1)} %copy-done.54), kind=kOutput, calls=%fused_computation.109 | convolution fusion | flops 150995040 | bytes 5243904 | tf_op jit(solution)/shard_map/hij,ijb->bh/dot_general | solution.py:241
  917.9 14.2 %psum.45 = f32[32,3]{0,1:T(4,128)} all-reduce(f32[32,3]{0,1:T(4,128)S(1)} %fusion.62), channel_id=1, replica_groups=mesh['dp'=8,'tensor'=4] {'dp'}, use_global_device_ids=true, to_apply=%region_31.32 | all-reduce | flops 96 | bytes 768 | tf_op jit(solution)/shard_map/psum | solution.py:266
  932.1 1.4 fusion.71
  933.5 39.2 %all-reduce = (f32[768]{0:T(1024)}, f32[768]{0:T(1024)}, f32[768,8]{0,1:T(8,128)}) all-reduce(f32[768]{0:T(1024)S(1)} %get-tuple-element.15, f32[768]{0:T(1024)S(1)} %get-tuple-element.11, f32[768,8]{0,1:T(8,128)S(1)} %fusion.109), channel_id=1, replica_groups=mesh['dp'=8,'tensor'=4] {'dp','tensor'}, use_global_device_ids=true, to_apply=%region_28.29 | all-reduce | flops 7680 | bytes 61440 | tf_op jit(solution)/shard_map/psum | solution.py:269
  972.7 2.7 fusion.68
  975.4 2.8 copy.73
  978.2 1.9 copy.74
  (220 shorter events, 17.9 us)
Async XLA Ops:
  7.2 447.0 %copy-start = (bf16[1,768,768]{2,1,0:T(8,128)(2,1)S(1)}, bf16[1,768,768]{2,1,0:T(8,128)(2,1)}, u32[]{:S(2)}) copy-start(bf16[1,768,768]{2,1,0:T(8,128)(2,1)} %param.26) | copy-start | bytes 3538948
  7.2 58.2 %all-gather.5.cloned.1.call-start = ((), (), s32[]{:S(2)}) async-start(), calls=%async_computation.8 | async-start | bytes 1966080 | tf_op jit(solution)/shard_map/all_gather | solution.py:92
  11.0 117.9 %reduce-scatter.5.cloned.1.call-start = ((), (), s32[]{:S(2)}) async-start(), calls=%async_computation.9 | async-start | bytes 1966080 | tf_op jit(solution)/shard_map/reduce_scatter | solution.py:118
  11.9 28.0 %copy-start.53 = (s32[32]{0:T(128)}, s32[32]{0:T(128)S(1)}, u32[]{:S(2)}) copy-start(s32[32]{0:T(128)S(1)} %convert_reduce_fusion) | copy-start | bytes 388
  12.2 26.0 %copy-start.25 = (s32[512,1024]{1,0:T(8,128)}, s32[512,1024]{1,0:T(8,128)S(1)}, u32[]{:S(2)}) copy-start(s32[512,1024]{1,0:T(8,128)S(1)} %fusion.29) | copy-start | bytes 6291460
  12.3 27.6 %copy-start.61 = (s32[32]{0:T(128)}, s32[32]{0:T(128)S(1)}, u32[]{:S(2)}) copy-start(s32[32]{0:T(128)S(1)} %pad_add_fusion) | copy-start | bytes 388
  12.3 26.2 %copy-start.52 = (s32[1024]{0:T(1024)S(1)}, s32[1024]{0:T(1024)}, u32[]{:S(2)}) copy-start(s32[1024]{0:T(1024)} %param.15) | copy-start | bytes 12292
  12.3 27.6 %copy-start.60 = (f32[32,3]{0,1:T(4,128)S(1)}, f32[32,3]{0,1:T(4,128)}, u32[]{:S(2)}) copy-start(f32[32,3]{0,1:T(4,128)} %param.21) | copy-start | bytes 1156
  39.9 45.1 %copy-start.8 = (pred[512,1024]{1,0:T(8,128)(4,1)}, pred[512,1024]{1,0:T(8,128)(4,1)S(1)}, u32[]{:S(2)}) copy-start(pred[512,1024]{1,0:T(8,128)(4,1)S(1)} %get-tuple-element.36) | copy-start | bytes 1572868
  39.9 46.7 %copy-start.10 = (pred[512,1024]{1,0:T(8,128)(4,1)}, pred[512,1024]{1,0:T(8,128)(4,1)S(1)}, u32[]{:S(2)}) copy-start(pred[512,1024]{1,0:T(8,128)(4,1)S(1)} %get-tuple-element.35) | copy-start | bytes 1572868
  39.9 25.4 %copy-start.58 = (bf16[768,3,192]{0,2,1:T(8,128)(2,1)S(1)}, bf16[768,3,192]{0,2,1:T(8,128)(2,1)}, u32[]{:S(2)}) copy-start(bf16[768,3,192]{0,2,1:T(8,128)(2,1)} %param.19) | copy-start | bytes 2654212
  68.0 10.1 %copy-start.14 = (bf16[1024,192]{0,1:T(8,128)(2,1)}, bf16[1024,192]{0,1:T(8,128)(2,1)S(1)}, u32[]{:S(2)}) copy-start(bf16[1024,192]{0,1:T(8,128)(2,1)S(1)} %get-tuple-element.27) | copy-start | bytes 1179652
  68.0 18.7 %copy-start.21 = (bf16[1024,192]{0,1:T(8,128)(2,1)}, bf16[1024,192]{0,1:T(8,128)(2,1)S(1)}, u32[]{:S(2)}) copy-start(bf16[1024,192]{0,1:T(8,128)(2,1)S(1)} %get-tuple-element.28) | copy-start | bytes 1179652
  68.0 8.5 copy-start.23
  68.0 10.0 %copy-start.28 = (bf16[512,192]{0,1:T(8,128)(2,1)}, bf16[512,192]{0,1:T(8,128)(2,1)S(1)}, u32[]{:S(2)}) copy-start(bf16[512,192]{0,1:T(8,128)(2,1)S(1)} %get-tuple-element.25) | copy-start | bytes 589828
  68.0 10.0 %slice-start.4 = ((s8[8388608]{0:T(1024)(128)(4,1)}), s8[4194304]{0:T(1024)(128)(4,1)S(1)}, s32[]{:S(2)}) async-start(s8[8388608]{0:T(1024)(128)(4,1)} %bitcast.149), calls=%async_computation.21 | async-start | bytes 8388608
  68.0 10.0 %slice-start.5 = ((s8[8388608]{0:T(1024)(128)(4,1)}), s8[4194304]{0:T(1024)(128)(4,1)S(1)}, s32[]{:S(2)}) async-start(s8[8388608]{0:T(1024)(128)(4,1)} %bitcast.149), calls=%async_computation.22 | async-start | bytes 8388608
  76.5 8.6 copy-start.4
  78.0 7.0 copy-start.42
  86.7 4.5 copy-start.18
  88.2 40.7 %copy-start.12 = (bf16[256,768]{1,0:T(8,128)(2,1)S(1)}, bf16[256,768]{1,0:T(8,128)(2,1)}, u32[]{:S(2)}) copy-start(bf16[256,768]{1,0:T(8,128)(2,1)} %param.14) | copy-start | bytes 1179652
  88.2 41.9 %copy-start.46 = (f32[768]{0:T(1024)S(1)}, f32[768]{0:T(1024)}, u32[]{:S(2)}) copy-start(f32[768]{0:T(1024)} %param.22) | copy-start | bytes 9220
  88.2 43.1 %copy-start.47 = (bf16[768,8]{0,1:T(8,128)(2,1)S(1)}, bf16[768,8]{0,1:T(8,128)(2,1)}, u32[]{:S(2)}) copy-start(bf16[768,8]{0,1:T(8,128)(2,1)} %param.23) | copy-start | bytes 36868
  90.7 171.5 %all-gather.7.cloned.1.call-start = ((), (), s32[]{:S(2)}) async-start(), calls=%async_computation.10 | async-start | bytes 7864320 | tf_op jit(solution)/shard_map/all_gather | solution.py:22
  131.3 5.8 copy-start.2
  147.8 230.0 %all-gather.9.cloned.1.call-start = ((), (), s32[]{:S(2)}) async-start(), calls=%async_computation.12 | async-start | bytes 7864320 | tf_op jit(solution)/shard_map/all_gather | solution.py:22
  262.2 115.6 %all-to-all-start = ((bf16[8,512,768]{2,1,0:T(8,128)(2,1)}), bf16[8,512,768]{2,1,0:T(8,128)(2,1)}, u32[]{:S(2)}, u32[]{:S(2)}) async-start(bf16[8,512,768]{2,1,0:T(8,128)(2,1)} %all-gather.7.cloned.1.call-done), calls=%async_computation.1 | async-start | bytes 12582912 | tf_op jit(solution)/shard_map/all_to_all | solution.py:23
  377.8 76.4 %all-to-all-start.2 = ((bf16[8,512,768]{2,1,0:T(8,128)(2,1)}), bf16[8,512,768]{2,1,0:T(8,128)(2,1)}, u32[]{:S(2)}, u32[]{:S(2)}) async-start(bf16[8,512,768]{2,1,0:T(8,128)(2,1)} %all-gather.9.cloned.1.call-done), calls=%async_computation.4 | async-start | bytes 12582912 | tf_op jit(solution)/shard_map/all_to_all | solution.py:23
  382.6 280.4 %reduce-scatter.7.cloned.1.call-start = ((), (), s32[]{:S(2)}) async-start(), calls=%async_computation.11 | async-start | bytes 7864320 | tf_op jit(solution)/shard_map/reduce_scatter | solution.py:28
  382.6 10.4 %copy-start.56 = (bf16[1,768,768]{2,1,0:T(8,128)(2,1)S(1)}, bf16[1,768,768]{2,1,0:T(8,128)(2,1)}, u32[]{:S(2)}) copy-start(bf16[1,768,768]{2,1,0:T(8,128)(2,1)} %param.24) | copy-start | bytes 3538948
  475.5 5.3 copy-start.63
  555.7 220.8 %reduce-scatter.9.cloned.1.call-start = ((), (), s32[]{:S(2)}) async-start(), calls=%async_computation.13 | async-start | bytes 7864320 | tf_op jit(solution)/shard_map/reduce_scatter | solution.py:28
  555.7 11.8 %copy-start.57 = (bf16[1,768,768]{2,1,0:T(8,128)(2,1)S(1)}, bf16[1,768,768]{2,1,0:T(8,128)(2,1)}, u32[]{:S(2)}) copy-start(bf16[1,768,768]{2,1,0:T(8,128)(2,1)} %param.25) | copy-start | bytes 3538948
  652.5 178.1 %all-gather.11.cloned.1.call-start = ((), (), s32[]{:S(2)}) async-start(), calls=%async_computation.14 | async-start | bytes 1966080 | tf_op jit(solution)/shard_map/all_gather | solution.py:202
  779.8 11.5 %copy-start.13 = (bf16[256,768]{1,0:T(8,128)(2,1)S(1)}, bf16[256,768]{1,0:T(8,128)(2,1)}, u32[]{:S(2)}) copy-start(bf16[256,768]{1,0:T(8,128)(2,1)} %reduce-scatter.5.cloned.1.call-done) | copy-start | bytes 1179652
  784.9 6.9 copy-start.19
  792.9 139.2 %reduce-scatter.11.cloned.1.call-start = ((), (), s32[]{:S(2)}) async-start(), calls=%async_computation.15 | async-start | bytes 1966080 | tf_op jit(solution)/shard_map/reduce_scatter | solution.py:255
  803.2 27.5 %copy-start.41 = (bf16[192,768]{1,0:T(8,128)(2,1)S(1)}, bf16[192,768]{1,0:T(8,128)(2,1)}, u32[]{:S(2)}) copy-start(bf16[192,768]{1,0:T(8,128)(2,1)} %param.20) | copy-start | bytes 884740
  803.2 29.6 %copy-start.11 = (pred[512,1024]{1,0:T(8,128)(4,1)S(1)}, pred[512,1024]{1,0:T(8,128)(4,1)}, u32[]{:S(2)}) copy-start(pred[512,1024]{1,0:T(8,128)(4,1)} %copy-done.10) | copy-start | bytes 1572868
  803.2 29.6 %copy-start.22 = (bf16[1024,192]{0,1:T(8,128)(2,1)S(1)}, bf16[1024,192]{0,1:T(8,128)(2,1)}, u32[]{:S(2)}) copy-start(bf16[1024,192]{0,1:T(8,128)(2,1)} %copy-done.21) | copy-start | bytes 1179652
  803.2 29.6 %copy-start.45 = (f32[3,512]{1,0:T(4,128)S(1)}, f32[3,512]{1,0:T(4,128)}, u32[]{:S(2)}) copy-start(f32[3,512]{1,0:T(4,128)} %copy-done.44) | copy-start | bytes 18436
  832.8 6.5 copy-start.31
  832.8 6.5 copy-start.29
  832.8 6.5 copy-start.9
  832.8 6.5 copy-start.43
  832.9 12.8 %slice-start = ((s8[6291456]{0:T(1024)(128)(4,1)}), s8[4194304]{0:T(1024)(128)(4,1)S(1)}, s32[]{:S(2)}) async-start(s8[6291456]{0:T(1024)(128)(4,1)} %bitcast.137), calls=%async_computation.17 | async-start | bytes 8388608
  832.9 12.8 %slice-start.2 = ((s8[6291456]{0:T(1024)(128)(4,1)}), s8[4194304]{0:T(1024)(128)(4,1)S(1)}, s32[]{:S(2)}) async-start(s8[6291456]{0:T(1024)(128)(4,1)} %bitcast.139), calls=%async_computation.19 | async-start | bytes 8388608
  839.3 6.4 slice-start.1
  839.3 6.4 slice-start.3
  853.2 9.5 copy-start.6
  853.2 7.0 copy-start.32
  857.4 4.2 copy-start.15
  867.6 10.6 %copy-start.3 = (bf16[256,768]{1,0:T(8,128)(2,1)S(1)}, bf16[256,768]{1,0:T(8,128)(2,1)}, u32[]{:S(2)}) copy-start(bf16[256,768]{1,0:T(8,128)(2,1)} %copy-done.2) | copy-start | bytes 1179652
  867.6 10.7 %copy-start.35 = (bf16[3,64,512]{2,1,0:T(8,128)(2,1)S(1)}, bf16[3,64,512]{2,1,0:T(8,128)(2,1)}, u32[]{:S(2)}) copy-start(bf16[3,64,512]{2,1,0:T(8,128)(2,1)} %copy-done.34) | copy-start | bytes 589828
  867.6 10.7 %copy-start.37 = (bf16[3,64,512]{2,1,0:T(8,128)(2,1)S(1)}, bf16[3,64,512]{2,1,0:T(8,128)(2,1)}, u32[]{:S(2)}) copy-start(bf16[3,64,512]{2,1,0:T(8,128)(2,1)} %copy-done.36) | copy-start | bytes 589828
  867.6 12.0 %copy-start.39 = (bf16[3,64,1024]{2,1,0:T(8,128)(2,1)S(1)}, bf16[3,64,1024]{2,1,0:T(8,128)(2,1)}, u32[]{:S(2)}) copy-start(bf16[3,64,1024]{2,1,0:T(8,128)(2,1)} %copy-done.38) | copy-start | bytes 1179652
  867.7 107.7 %all-reduce.4.cloned.1.call-start = ((), (), s32[]{:S(2)}) async-start(), calls=%async_computation.16 | async-start | bytes 4718592 | tf_op jit(solution)/shard_map/psum | solution.py:266
  867.7 10.7 %copy-start.33 = (bf16[1024,768]{1,0:T(8,128)(2,1)S(1)}, bf16[1024,768]{1,0:T(8,128)(2,1)}, u32[]{:S(2)}) copy-start(bf16[1024,768]{1,0:T(8,128)(2,1)} %all-gather.11.cloned.1.call-done) | copy-start | bytes 4718596
  867.7 12.0 %copy-start.55 = (bf16[1024,768]{1,0:T(8,128)(2,1)S(1)}, bf16[1024,768]{1,0:T(8,128)(2,1)}, u32[]{:S(2)}) copy-start(bf16[1024,768]{1,0:T(8,128)(2,1)} %all-gather.5.cloned.1.call-done) | copy-start | bytes 4718596
  900.2 31.9 %copy-start.48 = (f32[768]{0:T(1024)S(1)}, f32[768]{0:T(1024)}, u32[]{:S(2)}) copy-start(f32[768]{0:T(1024)} %param.18) | copy-start | bytes 9220
  900.2 31.9 %copy-start.51 = (f32[256]{0:T(256)S(1)}, f32[256]{0:T(256)}, u32[]{:S(2)}) copy-start(f32[256]{0:T(256)} %copy-done.50) | copy-start | bytes 3076
  900.2 72.5 %copy-start.17 = (f32[256,768]{1,0:T(8,128)S(1)}, f32[256,768]{1,0:T(8,128)}, u32[]{:S(2)}) copy-start(f32[256,768]{1,0:T(8,128)} %copy-done.16) | copy-start | bytes 2359300
  900.2 72.5 %copy-start.20 = (bf16[256,768]{1,0:T(8,128)(2,1)S(1)}, bf16[256,768]{1,0:T(8,128)(2,1)}, u32[]{:S(2)}) copy-start(bf16[256,768]{1,0:T(8,128)(2,1)} %param.27) | copy-start | bytes 1179652
  900.2 79.9 %copy-start.1 = (bf16[1,768,768]{2,1,0:T(8,128)(2,1)S(1)}, bf16[1,768,768]{2,1,0:T(8,128)(2,1)}, u32[]{:S(2)}) copy-start(bf16[1,768,768]{2,1,0:T(8,128)(2,1)} %param.26) | copy-start | bytes 3538948
  (17 other events, 38.5 us)
Sparse Core Ops, SparseCore 0:
  11.1 39.7 all-gather.4
  90.8 38.0 reduce-scatter.4
  147.9 114.2 all-gather.6
  264.2 113.5 all-gather.8
  555.8 107.1 reduce-scatter.6
  665.1 111.2 reduce-scatter.8
  793.0 37.6 all-gather.10
  867.7 34.1 reduce-scatter.10
  905.8 62.1 all-reduce.3
where the time goes:
time: 996 us; the launch traced here: 987 us
  waiting for transfers between devices  429 us (43%)
  matrix products  241 us (24%)
  blocking collectives  203 us (20%)
  other arithmetic  46.1 us (5%)
  local copies, waits for them, and re-layouts  42.7 us (4%)
  between operations  15.4 us (2%)
  starting transfers between devices  9.99 us (1%)
    all_gather x2, waiting for transfers between devices, carry_out(): grouped = lax.all_gather(buffer, 'tensor', axis=1, tiled=True)  225 us
    all_to_all x2, blocking collectives, carry_back(): lax.all_to_all(partial_rows, 'dp', split_axis=0, concat_axis=0, tiled=True)  150 us
    reduce_scatter x2, waiting for transfers between devices, carry_back(): lax.psum_scatter(returned.astype(jnp.float32).astype(jnp.bfloat16), 'tens...  107 us
    dot_general x12, matrix products, contract(): lax.dot_general(left, right, (((left_dim,), (right_dim,)), ((), ())), pre...  82.9 us
    dot_general x2, matrix products, block_scores(): bias = jnp.einsum('ijb,bh->hij', onehot, rel_bias, precision=HIGHEST)  51.3 us
    all_to_all x2, waiting for transfers between devices, carry_out(): lax.all_to_all(grouped, 'dp', split_axis=0, concat_axis=0, tiled=True)  50.6 us
    psum x1, blocking collectives, local(): lax.psum((grad_router, grad_norm_two, grad_norm_one), ('dp', 'tensor'))  39.2 us
    dot_general x2, matrix products, local(): jnp.einsum('hij,ijb->bh', grad_scores.astype(jnp.float32), onehot, precis...  34.9 us
  transfers between devices with their start and end apart: 11, of which 7 were waited for; matrix products, arithmetic and copies ran while one was open for 20% of the time, Pallas kernels for 0%

commit v1 on v0

--- a/solution.py
+++ b/solution.py
@@ -8,6 +8,18 @@
 HIGHEST = lax.Precision.HIGHEST
 
 
+def doubled_up(array, axis, dim):
+    ways, here = (lax.axis_size(axis), lax.axis_index(axis))
+    grown, reach = (array, 1)
+    while reach < ways:
+        theirs = lax.ppermute(grown, axis, [(d, d ^ reach) for d in range(ways)])
+        mine_first = jnp.concatenate([grown, theirs], axis=dim)
+        theirs_first = jnp.concatenate([theirs, grown], axis=dim)
+        grown = jnp.where(here & reach == 0, mine_first, theirs_first)
+        reach = 2 * reach
+    return grown
+
+
 def contract(left, right, left_dim, right_dim):
     return lax.dot_general(
         left, right, (((left_dim,), (right_dim,)), ((), ())), preferred_element_type=jnp.float32
@@ -19,7 +31,7 @@
 
 
 def carry_out(buffer):
-    grouped = lax.all_gather(buffer, "tensor", axis=1, tiled=True)
+    grouped = doubled_up(buffer, "tensor", 1)
     return lax.all_to_all(grouped, "dp", split_axis=0, concat_axis=0, tiled=True)
 
 

time: 996 us -> 1110 us (1.11)
  waiting for transfers between devices: 429 us -> 515 us
  other arithmetic: 46.1 us -> 67.7 us
    ppermute x0 -> x4, waiting for transfers between devices: none -> 309 us  [doubled_up(): theirs = lax.ppermute(grown, axis, [(d, d ^ reach) for d in range(ways)])]
    all_gather x2 -> x0, waiting for transfers between devices: 225 us -> none  [carry_out(): grouped = lax.all_gather(buffer, 'tensor', axis=1, tiled=True)]
    select_n x0 -> x4, other arithmetic: none -> 21.6 us  [doubled_up(): grown = jnp.where(here & reach == 0, mine_first, theirs_first)]
  transfers between devices with their start and end apart: 11 -> 13, of which waited for: 7 -> 8; matrix products, arithmetic and copies ran while one was open for 20% -> 19% of each run, Pallas kernels for 0% -> 0%
where the time goes in v1:
time: 1110 us; the launch traced here: 1100 us
  waiting for transfers between devices  515 us (46%)
  matrix products  239 us (22%)
  blocking collectives  203 us (18%)
  other arithmetic  67.7 us (6%)
  local copies, waits for them, and re-layouts  42.7 us (4%)
  between operations  15.7 us (1%)
  starting transfers between devices  13.1 us (1%)
    ppermute x4, waiting for transfers between devices, doubled_up(): theirs = lax.ppermute(grown, axis, [(d, d ^ reach) for d in range(ways)])  309 us
    all_to_all x2, blocking collectives, carry_back(): lax.all_to_all(partial_rows, 'dp', split_axis=0, concat_axis=0, tiled=True)  150 us
    reduce_scatter x2, waiting for transfers between devices, carry_back(): lax.psum_scatter(returned.astype(jnp.float32).astype(jnp.bfloat16), 'tens...  109 us
    dot_general x12, matrix products, contract(): lax.dot_general(left, right, (((left_dim,), (right_dim,)), ((), ())), pre...  81.6 us
    dot_general x2, matrix products, block_scores(): bias = jnp.einsum('ijb,bh->hij', onehot, rel_bias, precision=HIGHEST)  51.3 us
    all_to_all x2, waiting for transfers between devices, carry_out(): lax.all_to_all(grouped, 'dp', split_axis=0, concat_axis=0, tiled=True)  50.7 us
    psum x1, blocking collectives, local(): lax.psum((grad_router, grad_norm_two, grad_norm_one), ('dp', 'tensor'))  39.2 us
    dot_general x2, matrix products, local(): jnp.einsum('hij,ijb->bh', grad_scores.astype(jnp.float32), onehot, precis...  34.9 us
  transfers between devices with their start and end apart: 13, of which 8 were waited for; matrix products, arithmetic and copies ran while one was open for 19% of the time, Pallas kernels for 0%

profile of v1, /device:TPU:0, one launch (start us, length us, event | category | flops | bytes accessed | tf_op | source)
XLA Modules:
  0.0 1096.5 jit_solution(9813510297868350629)
XLA Ops:
  9.1 1.9 fusion.69
  12.3 25.9 %fusion.3 = f32[512,1024,3]{1,2,0:T(4,128)} fusion(s32[512,1024]{1,0:T(8,128)S(1)} %fusion.29, s32[32]{0:T(128)S(1)} %pad_add_fusion, s32[32]{0:T(128)S(1)} %convert_reduce_fusion, f32[32,3]{0,1:T(4,128)} %param.21), kind=kOutput, calls=%fused_computation.10 | convolution fusion | flops 654311424 | bytes 8389248 | tf_op jit(solution)/shard_map/ijb,bh->hij/dot_general | solution.py:61
  39.9 25.4 %fusion.1 = f32[512,1024,3]{1,2,0:T(4,128)} fusion(s32[512,1024]{1,0:T(8,128)S(1)} %fusion.31, s32[32]{0:T(128)S(1)} %pad_add_fusion, s32[32]{0:T(128)S(1)} %convert_reduce_fusion, f32[32,3]{0,1:T(4,128)S(1)} %copy-done.60), kind=kOutput, calls=%fused_computation.8 | convolution fusion | flops 654311424 | bytes 8389248 | tf_op jit(solution)/shard_map/ijb,bh->hij/dot_general | solution.py:61
  65.4 2.5 convolution_convert_fusion.3
  68.1 8.4 fusion.105
  78.1 5.0 fusion.106
  83.1 1.9 exponential_reduce_fusion.1
  88.9 1.8 convolution_convert_fusion.2
  91.1 1.5 mul.287
  92.7 3.1 mul.288
  97.6 2.4 scatter_custom_fusion
  100.1 28.7 %reduce-scatter.5.cloned.1.call-done = bf16[256,768]{1,0:T(8,128)(2,1)} async-done(((bf16[1024,768]{1,0:T(8,128)(2,1)}), bf16[256,768]{1,0:T(8,128)(2,1)}) %reduce-scatter.5.cloned.1.call-update) | async-done | bytes 393232 | tf_op jit(solution)/shard_map/reduce_scatter | solution.py:130
  131.9 5.2 gather_fusion
  137.1 1.6 multiply_convert_fusion.4
  138.7 5.2 gather_fusion.2
  143.9 3.8 broadcast_select_fusion
  148.0 35.9 %collective-permute-done = bf16[8,128,768]{2,1,0:T(8,128)(2,1)} collective-permute-done((bf16[8,128,768]{2,1,0:T(8,128)(2,1)}, bf16[8,128,768]{2,1,0:T(8,128)(2,1)}, u32[]{:S(2)}, u32[]{:S(2)}) %collective-permute-start) | collective-permute-done | bytes 1572896 | tf_op jit(solution)/shard_map/ppermute | solution.py:15
  184.0 5.0 maximum_select_fusion.2
  188.9 1.6 collective-permute-start.1
  191.0 134.9 %collective-permute-done.1 = bf16[8,256,768]{2,1,0:T(8,128)(2,1)} collective-permute-done((bf16[8,256,768]{2,1,0:T(8,128)(2,1)}, bf16[8,256,768]{2,1,0:T(8,128)(2,1)}, u32[]{:S(2)}, u32[]{:S(2)}) %collective-permute-start.1) | collective-permute-done | bytes 3145760 | tf_op jit(solution)/shard_map/ppermute | solution.py:15
  326.0 8.9 maximum_select_fusion
  334.9 4.8 all-to-all-start
  339.7 3.6 maximum_select_fusion.3
  343.4 138.1 %collective-permute-done.3 = bf16[8,256,768]{2,1,0:T(8,128)(2,1)S(1)} collective-permute-done((bf16[8,256,768]{2,1,0:T(8,128)(2,1)S(1)}, bf16[8,256,768]{2,1,0:T(8,128)(2,1)S(1)}, u32[]{:S(2)}, u32[]{:S(2)}) %collective-permute-start.3) | collective-permute-done | bytes 3145760 | tf_op jit(solution)/shard_map/ppermute | solution.py:15
  481.5 4.1 maximum_select_fusion.1
  485.6 5.0 all-to-all-start.2
  490.6 10.2 fusion.46
  500.9 10.5 fusion.50
  511.4 50.7 %all-to-all-done.2 = bf16[8,512,768]{2,1,0:T(8,128)(2,1)} async-done(((bf16[8,512,768]{2,1,0:T(8,128)(2,1)}), bf16[8,512,768]{2,1,0:T(8,128)(2,1)}, u32[]{:S(2)}, u32[]{:S(2)}) %all-to-all-start.2) | async-done | bytes 6291488 | tf_op jit(solution)/shard_map/all_to_all | solution.py:35
  562.2 21.4 %multiply_convert_fusion = (bf16[4096,768]{1,0:T(8,128)(2,1)}, bf16[4096,768]{1,0:T(8,128)(2,1)}, bf16[4096,768]{1,0:T(8,128)(2,1)S(1)}) fusion(f32[4096,768]{1,0:T(8,128)} %fusion.50, f32[4096,768]{1,0:T(8,128)} %fusion.46, bf16[4096,768]{1,0:T(8,128)(2,1)} %bitcast.25, bf16[1,768,768]{2,1,0:T(8,128)(2,1)S(1)} %copy-done), kind=kOutput, calls=%fused_computation.33 | convolution fusion | flops 4913627136 | bytes 51511296 | tf_op jit(solution)/shard_map/dot_general | solution.py:24
  583.6 5.3 convolution_convert_fusion
  588.8 74.9 %all_to_all.20 = bf16[8,512,768]{2,1,0:T(8,128)(2,1)} all-to-all(bf16[8,512,768]{2,1,0:T(8,128)(2,1)S(1)} %bitcast.146), channel_id=1, replica_groups=mesh['dp'=8,'tensor'=4] {'dp'}, dimensions={0} | all-to-all | bytes 12582912 | tf_op jit(solution)/shard_map/all_to_all | solution.py:39
  664.2 10.7 fusion.48
  675.0 10.0 add_convert_fusion
  684.9 74.9 %all_to_all.21 = bf16[8,512,768]{2,1,0:T(8,128)(2,1)} all-to-all(bf16[8,512,768]{2,1,0:T(8,128)(2,1)S(1)} %bitcast.145), channel_id=1, replica_groups=mesh['dp'=8,'tensor'=4] {'dp'}, dimensions={0} | all-to-all | bytes 12582912 | tf_op jit(solution)/shard_map/all_to_all | solution.py:39
  760.0 12.2 %reduce-scatter.7.cloned.1.call-done = bf16[8,128,768]{2,1,0:T(8,128)(2,1)} async-done(((bf16[8,512,768]{2,1,0:T(8,128)(2,1)}), bf16[8,128,768]{2,1,0:T(8,128)(2,1)}) %reduce-scatter.7.cloned.1.call-update) | async-done | bytes 1572880 | tf_op jit(solution)/shard_map/reduce_scatter | solution.py:40
  772.2 3.3 bitcast_convert_fusion.1
  775.5 5.1 gather_fusion.1
  780.5 3.3 reshape.354
  783.9 5.0 multiply_reduce_fusion.2
  789.0 96.6 %reduce-scatter.9.cloned.1.call-done = bf16[8,128,768]{2,1,0:T(8,128)(2,1)} async-done(((bf16[8,512,768]{2,1,0:T(8,128)(2,1)}), bf16[8,128,768]{2,1,0:T(8,128)(2,1)}) %reduce-scatter.9.cloned.1.call-update) | async-done | bytes 1572880 | tf_op jit(solution)/shard_map/reduce_scatter | solution.py:40
  885.6 3.3 bitcast_convert_fusion
  889.0 5.1 gather_fusion.3
  894.1 3.1 reshape.359
  897.2 3.3 reduce_sum.183
  902.3 10.1 convolution_bitcast_fusion
  912.4 10.1 convolution_bitcast_fusion.1
  922.5 17.3 %all-gather.5.cloned.1.call-done = bf16[1024,768]{1,0:T(8,128)(2,1)} async-done(((bf16[256,768]{1,0:T(8,128)(2,1)}), bf16[1024,768]{1,0:T(8,128)(2,1)}) %all-gather.5.cloned.1.call-update) | async-done | bytes 1572880 | tf_op jit(solution)/shard_map/all_gather | solution.py:214
  939.9 2.1 convolution_convert_fusion.4
  942.1 6.4 multiply_reduce_fusion.1
  948.5 6.3 multiply_reduce_fusion
  954.9 7.5 multiply_convert_fusion.2
  962.4 4.2 fusion.55
  966.6 2.7 fusion.108
  974.2 2.6 convolution_convert_fusion.1
  976.9 10.5 convolution_bitcast_fusion.2
  988.9 2.3 fusion.74
  992.1 17.2 %fusion.56 = f32[32,3]{0,1:T(4,128)S(1)} fusion(bf16[3,512,1024]{2,1,0:T(8,128)(2,1)S(1)} %copy-done.7, s32[512,1024]{1,0:T(8,128)S(1)} %copy-done.26, s32[32]{0:T(128)S(1)} %copy-done.62, s32[32]{0:T(128)S(1)} %copy-done.54), kind=kOutput, calls=%fused_computation.111 | convolution fusion | flops 150994944 | bytes 5243520 | tf_op jit(solution)/shard_map/hij,ijb->bh/dot_general | solution.py:253
  1009.4 17.7 %fusion.62 = f32[32,3]{0,1:T(4,128)S(1)} fusion(f32[32,3]{0,1:T(4,128)S(1)} %fusion.56, bf16[3,512,1024]{2,1,0:T(8,128)(2,1)} %get-tuple-element.53, s32[512,1024]{1,0:T(8,128)} %copy-done.27, s32[32]{0:T(128)S(1)} %copy-done.62, s32[32]{0:T(128)S(1)} %copy-done.54), kind=kOutput, calls=%fused_computation.113 | convolution fusion | flops 150995040 | bytes 5243904 | tf_op jit(solution)/shard_map/hij,ijb->bh/dot_general | solution.py:253
  1027.1 14.2 %psum.45 = f32[32,3]{0,1:T(4,128)} all-reduce(f32[32,3]{0,1:T(4,128)S(1)} %fusion.62), channel_id=1, replica_groups=mesh['dp'=8,'tensor'=4] {'dp'}, use_global_device_ids=true, to_apply=%region_31.32 | all-reduce | flops 96 | bytes 768 | tf_op jit(solution)/shard_map/psum | solution.py:278
  1042.6 39.2 %all-reduce = (f32[768]{0:T(1024)}, f32[768]{0:T(1024)}, f32[768,8]{0,1:T(8,128)}) all-reduce(f32[768]{0:T(1024)S(1)} %get-tuple-element.15, f32[768]{0:T(1024)S(1)} %get-tuple-element.11, f32[768,8]{0,1:T(8,128)S(1)} %fusion.109), channel_id=1, replica_groups=mesh['dp'=8,'tensor'=4] {'dp','tensor'}, use_global_device_ids=true, to_apply=%region_28.29 | all-reduce | flops 7680 | bytes 61440 | tf_op jit(solution)/shard_map/psum | solution.py:281
  1081.8 2.7 fusion.68
  1084.5 2.8 copy.73
  1087.3 1.9 copy.74
  (226 shorter events, 27.6 us)
Async XLA Ops:
  7.2 555.0 %copy-start = (bf16[1,768,768]{2,1,0:T(8,128)(2,1)S(1)}, bf16[1,768,768]{2,1,0:T(8,128)(2,1)}, u32[]{:S(2)}) copy-start(bf16[1,768,768]{2,1,0:T(8,128)(2,1)} %param.26) | copy-start | bytes 3538948
  7.2 58.2 %all-gather.3.cloned.1.call-start = ((), (), s32[]{:S(2)}) async-start(), calls=%async_computation.8 | async-start | bytes 1966080 | tf_op jit(solution)/shard_map/all_gather | solution.py:104
  11.0 117.9 %reduce-scatter.5.cloned.1.call-start = ((), (), s32[]{:S(2)}) async-start(), calls=%async_computation.9 | async-start | bytes 1966080 | tf_op jit(solution)/shard_map/reduce_scatter | solution.py:130
  11.9 28.0 %copy-start.53 = (s32[32]{0:T(128)}, s32[32]{0:T(128)S(1)}, u32[]{:S(2)}) copy-start(s32[32]{0:T(128)S(1)} %convert_reduce_fusion) | copy-start | bytes 388
  12.2 26.0 %copy-start.25 = (s32[512,1024]{1,0:T(8,128)}, s32[512,1024]{1,0:T(8,128)S(1)}, u32[]{:S(2)}) copy-start(s32[512,1024]{1,0:T(8,128)S(1)} %fusion.29) | copy-start | bytes 6291460
  12.3 27.6 %copy-start.61 = (s32[32]{0:T(128)}, s32[32]{0:T(128)S(1)}, u32[]{:S(2)}) copy-start(s32[32]{0:T(128)S(1)} %pad_add_fusion) | copy-start | bytes 388
  12.3 26.2 %copy-start.52 = (s32[1024]{0:T(1024)S(1)}, s32[1024]{0:T(1024)}, u32[]{:S(2)}) copy-start(s32[1024]{0:T(1024)} %param.15) | copy-start | bytes 12292
  12.3 27.6 %copy-start.60 = (f32[32,3]{0,1:T(4,128)S(1)}, f32[32,3]{0,1:T(4,128)}, u32[]{:S(2)}) copy-start(f32[32,3]{0,1:T(4,128)} %param.21) | copy-start | bytes 1156
  39.9 45.2 %copy-start.8 = (pred[512,1024]{1,0:T(8,128)(4,1)}, pred[512,1024]{1,0:T(8,128)(4,1)S(1)}, u32[]{:S(2)}) copy-start(pred[512,1024]{1,0:T(8,128)(4,1)S(1)} %get-tuple-element.36) | copy-start | bytes 1572868
  39.9 46.7 %copy-start.10 = (pred[512,1024]{1,0:T(8,128)(4,1)}, pred[512,1024]{1,0:T(8,128)(4,1)S(1)}, u32[]{:S(2)}) copy-start(pred[512,1024]{1,0:T(8,128)(4,1)S(1)} %get-tuple-element.35) | copy-start | bytes 1572868
  39.9 25.4 %copy-start.58 = (bf16[768,3,192]{0,2,1:T(8,128)(2,1)S(1)}, bf16[768,3,192]{0,2,1:T(8,128)(2,1)}, u32[]{:S(2)}) copy-start(bf16[768,3,192]{0,2,1:T(8,128)(2,1)} %param.19) | copy-start | bytes 2654212
  68.0 10.1 copy-start.14
  68.0 18.7 %copy-start.21 = (bf16[1024,192]{0,1:T(8,128)(2,1)}, bf16[1024,192]{0,1:T(8,128)(2,1)S(1)}, u32[]{:S(2)}) copy-start(bf16[1024,192]{0,1:T(8,128)(2,1)S(1)} %get-tuple-element.28) | copy-start | bytes 1179652
  68.0 8.5 copy-start.23
  68.0 10.0 copy-start.28
  68.0 10.0 slice-start.4
  68.0 10.0 slice-start.5
  76.5 8.6 copy-start.4
  78.0 7.1 copy-start.42
  88.2 40.6 %copy-start.12 = (bf16[256,768]{1,0:T(8,128)(2,1)S(1)}, bf16[256,768]{1,0:T(8,128)(2,1)}, u32[]{:S(2)}) copy-start(bf16[256,768]{1,0:T(8,128)(2,1)} %param.14) | copy-start | bytes 1179652
  88.2 41.8 %copy-start.46 = (f32[768]{0:T(1024)S(1)}, f32[768]{0:T(1024)}, u32[]{:S(2)}) copy-start(f32[768]{0:T(1024)} %param.22) | copy-start | bytes 9220
  88.2 43.0 %copy-start.47 = (bf16[768,8]{0,1:T(8,128)(2,1)S(1)}, bf16[768,8]{0,1:T(8,128)(2,1)}, u32[]{:S(2)}) copy-start(bf16[768,8]{0,1:T(8,128)(2,1)} %param.23) | copy-start | bytes 36868
  131.3 5.8 copy-start.2
  147.7 36.3 %collective-permute-start = (bf16[8,128,768]{2,1,0:T(8,128)(2,1)}, bf16[8,128,768]{2,1,0:T(8,128)(2,1)}, u32[]{:S(2)}, u32[]{:S(2)}) collective-permute-start(bf16[8,128,768]{2,1,0:T(8,128)(2,1)} %get-tuple-element.40), channel_id=1, source_target_pairs={{0,1},{1,0},{2,3},{3,2},{4,5},{5,4},{6,7},{7,6},{8,9},{9,8},{10,11... | collective-permute-start | bytes 4718600 | tf_op jit(solution)/shard_map/ppermute | solution.py:15
  188.9 137.0 %collective-permute-start.1 = (bf16[8,256,768]{2,1,0:T(8,128)(2,1)}, bf16[8,256,768]{2,1,0:T(8,128)(2,1)}, u32[]{:S(2)}, u32[]{:S(2)}) collective-permute-start(bf16[8,256,768]{2,1,0:T(8,128)(2,1)} %maximum_select_fusion.2), channel_id=1, source_target_pairs={{0,2},{1,3},{2,0},{3,1},{4,6},{5,7},{6,4},{7,5},{8,10},{9,11},{10,... | collective-permute-start | bytes 9437192 | tf_op jit(solution)/shard_map/ppermute | solution.py:15
  190.5 149.1 %collective-permute-start.2 = (bf16[8,128,768]{2,1,0:T(8,128)(2,1)}, bf16[8,128,768]{2,1,0:T(8,128)(2,1)}, u32[]{:S(2)}, u32[]{:S(2)}) collective-permute-start(bf16[8,128,768]{2,1,0:T(8,128)(2,1)} %get-tuple-element.39), channel_id=1, source_target_pairs={{0,1},{1,0},{2,3},{3,2},{4,5},{5,4},{6,7},{7,6},{8,9},{9,8},{10,11... | collective-permute-start | bytes 4718600 | tf_op jit(solution)/shard_map/ppermute | solution.py:15
  334.9 150.7 %all-to-all-start = ((bf16[8,512,768]{2,1,0:T(8,128)(2,1)}), bf16[8,512,768]{2,1,0:T(8,128)(2,1)}, u32[]{:S(2)}, u32[]{:S(2)}) async-start(bf16[8,512,768]{2,1,0:T(8,128)(2,1)} %maximum_select_fusion), calls=%async_computation.1 | async-start | bytes 12582912 | tf_op jit(solution)/shard_map/all_to_all | solution.py:35
  343.3 138.2 %collective-permute-start.3 = (bf16[8,256,768]{2,1,0:T(8,128)(2,1)S(1)}, bf16[8,256,768]{2,1,0:T(8,128)(2,1)S(1)}, u32[]{:S(2)}, u32[]{:S(2)}) collective-permute-start(bf16[8,256,768]{2,1,0:T(8,128)(2,1)S(1)} %maximum_select_fusion.3), channel_id=1, source_target_pairs={{0,2},{1,3},{2,0},{3,1},{4,6},{5,7},{6,4},{7,5},{8,10},{9,11},{10,... | collective-permute-start | bytes 9437192 | tf_op jit(solution)/shard_map/ppermute | solution.py:15
  485.6 76.6 %all-to-all-start.2 = ((bf16[8,512,768]{2,1,0:T(8,128)(2,1)}), bf16[8,512,768]{2,1,0:T(8,128)(2,1)}, u32[]{:S(2)}, u32[]{:S(2)}) async-start(bf16[8,512,768]{2,1,0:T(8,128)(2,1)} %maximum_select_fusion.1), calls=%async_computation.4 | async-start | bytes 12582912 | tf_op jit(solution)/shard_map/all_to_all | solution.py:35
  490.6 281.6 %reduce-scatter.7.cloned.1.call-start = ((), (), s32[]{:S(2)}) async-start(), calls=%async_computation.10 | async-start | bytes 7864320 | tf_op jit(solution)/shard_map/reduce_scatter | solution.py:40
  490.6 10.3 copy-start.56
  583.6 5.3 copy-start.63
  663.8 221.8 %reduce-scatter.9.cloned.1.call-start = ((), (), s32[]{:S(2)}) async-start(), calls=%async_computation.11 | async-start | bytes 7864320 | tf_op jit(solution)/shard_map/reduce_scatter | solution.py:40
  664.2 10.7 copy-start.57
  759.9 180.0 %all-gather.5.cloned.1.call-start = ((), (), s32[]{:S(2)}) async-start(), calls=%async_computation.12 | async-start | bytes 1966080 | tf_op jit(solution)/shard_map/all_gather | solution.py:214
  889.0 11.5 %copy-start.13 = (bf16[256,768]{1,0:T(8,128)(2,1)S(1)}, bf16[256,768]{1,0:T(8,128)(2,1)}, u32[]{:S(2)}) copy-start(bf16[256,768]{1,0:T(8,128)(2,1)} %reduce-scatter.5.cloned.1.call-done) | copy-start | bytes 1179652
  894.1 6.9 copy-start.19
  902.1 139.2 %reduce-scatter.11.cloned.1.call-start = ((), (), s32[]{:S(2)}) async-start(), calls=%async_computation.13 | async-start | bytes 1966080 | tf_op jit(solution)/shard_map/reduce_scatter | solution.py:267
  912.4 27.5 %copy-start.41 = (bf16[192,768]{1,0:T(8,128)(2,1)S(1)}, bf16[192,768]{1,0:T(8,128)(2,1)}, u32[]{:S(2)}) copy-start(bf16[192,768]{1,0:T(8,128)(2,1)} %param.20) | copy-start | bytes 884740
  912.4 29.6 %copy-start.11 = (pred[512,1024]{1,0:T(8,128)(4,1)S(1)}, pred[512,1024]{1,0:T(8,128)(4,1)}, u32[]{:S(2)}) copy-start(pred[512,1024]{1,0:T(8,128)(4,1)} %copy-done.10) | copy-start | bytes 1572868
  912.4 29.6 %copy-start.22 = (bf16[1024,192]{0,1:T(8,128)(2,1)S(1)}, bf16[1024,192]{0,1:T(8,128)(2,1)}, u32[]{:S(2)}) copy-start(bf16[1024,192]{0,1:T(8,128)(2,1)} %copy-done.21) | copy-start | bytes 1179652
  912.4 29.6 %copy-start.45 = (f32[3,512]{1,0:T(4,128)S(1)}, f32[3,512]{1,0:T(4,128)}, u32[]{:S(2)}) copy-start(f32[3,512]{1,0:T(4,128)} %copy-done.44) | copy-start | bytes 18436
  942.0 6.5 copy-start.31
  942.0 6.5 copy-start.29
  942.0 6.5 copy-start.9
  942.0 6.5 copy-start.43
  942.0 12.8 %slice-start = ((s8[6291456]{0:T(1024)(128)(4,1)}), s8[4194304]{0:T(1024)(128)(4,1)S(1)}, s32[]{:S(2)}) async-start(s8[6291456]{0:T(1024)(128)(4,1)} %bitcast.137), calls=%async_computation.15 | async-start | bytes 8388608
  942.1 12.8 %slice-start.2 = ((s8[6291456]{0:T(1024)(128)(4,1)}), s8[4194304]{0:T(1024)(128)(4,1)S(1)}, s32[]{:S(2)}) async-start(s8[6291456]{0:T(1024)(128)(4,1)} %bitcast.139), calls=%async_computation.17 | async-start | bytes 8388608
  948.5 6.4 slice-start.1
  948.5 6.4 slice-start.3
  962.4 9.5 copy-start.6
  962.4 7.0 copy-start.32
  976.8 10.6 copy-start.3
  976.8 10.7 copy-start.35
  976.8 10.7 copy-start.37
  976.8 12.0 %copy-start.39 = (bf16[3,64,1024]{2,1,0:T(8,128)(2,1)S(1)}, bf16[3,64,1024]{2,1,0:T(8,128)(2,1)}, u32[]{:S(2)}) copy-start(bf16[3,64,1024]{2,1,0:T(8,128)(2,1)} %copy-done.38) | copy-start | bytes 1179652
  976.8 107.7 %all-reduce.4.cloned.1.call-start = ((), (), s32[]{:S(2)}) async-start(), calls=%async_computation.14 | async-start | bytes 4718592 | tf_op jit(solution)/shard_map/psum | solution.py:278
  976.9 10.7 copy-start.33
  976.9 12.0 %copy-start.55 = (bf16[1024,768]{1,0:T(8,128)(2,1)S(1)}, bf16[1024,768]{1,0:T(8,128)(2,1)}, u32[]{:S(2)}) copy-start(bf16[1024,768]{1,0:T(8,128)(2,1)} %all-gather.3.cloned.1.call-done) | copy-start | bytes 4718596
  1009.3 31.9 %copy-start.48 = (f32[768]{0:T(1024)S(1)}, f32[768]{0:T(1024)}, u32[]{:S(2)}) copy-start(f32[768]{0:T(1024)} %param.18) | copy-start | bytes 9220
  1009.3 31.9 %copy-start.51 = (f32[256]{0:T(256)S(1)}, f32[256]{0:T(256)}, u32[]{:S(2)}) copy-start(f32[256]{0:T(256)} %copy-done.50) | copy-start | bytes 3076
  1009.4 72.5 %copy-start.17 = (f32[256,768]{1,0:T(8,128)S(1)}, f32[256,768]{1,0:T(8,128)}, u32[]{:S(2)}) copy-start(f32[256,768]{1,0:T(8,128)} %copy-done.16) | copy-start | bytes 2359300
  1009.4 72.4 %copy-start.20 = (bf16[256,768]{1,0:T(8,128)(2,1)S(1)}, bf16[256,768]{1,0:T(8,128)(2,1)}, u32[]{:S(2)}) copy-start(bf16[256,768]{1,0:T(8,128)(2,1)} %param.27) | copy-start | bytes 1179652
  1009.4 79.9 %copy-start.1 = (bf16[1,768,768]{2,1,0:T(8,128)(2,1)S(1)}, bf16[1,768,768]{2,1,0:T(8,128)(2,1)}, u32[]{:S(2)}) copy-start(bf16[1,768,768]{2,1,0:T(8,128)(2,1)} %param.26) | copy-start | bytes 3538948
  (19 other events, 47.2 us)
Sparse Core Ops, SparseCore 0:
  11.1 39.7 all-gather.2
  90.8 37.9 reduce-scatter.4
  663.9 108.2 reduce-scatter.6
  774.3 111.2 reduce-scatter.8
  902.2 37.6 all-gather.4
  976.9 34.1 reduce-scatter.10
  1015.0 62.1 all-reduce.3
